TPU v7x, 32 devices: a whole 2x2x4 slice. The times are simulated.
32 devices in a mesh: vocab: 8 (over z, x), batch: 4 (over y, core).
Axes of the slice: x: 2, y: 2, z: 4, core: 2. Of those that a mesh axis runs over, the one named last changes fastest.
Arguments:
- hidden: bfloat16 [256, 1024], P(('vocab', 'batch'))
- embedding: bfloat16 [8192, 1024], P('vocab')
- block_counts: int32 [64], P('vocab'), may hold values from 1 to 4095
- lang_blocks: int32 [200, 64], replicated, may hold values from -1 to 63, as said below
- sent_lang: int32 [4], replicated, may hold values from 0 to 199
- targets: int32 [256], replicated, may hold values from 0 to 8191, as said below
Outputs:
- token_loss: float32 [256], P(('vocab', 'batch'))
- grad_embed: bfloat16 [8192, 1024], P(('vocab', 'batch'))
Inputs may be any that keep to these rules, and one draw needn't show every extreme that they name: `lang_blocks`: each list holds distinct block numbers and then -1 padding; the first entry of every list is block 0; at least 16 entries are blocks, and some language fills all 64 entries. `targets`: the target of token t lies in a block listed for the language of sentence t // 64.
All inputs are finite; a program needn't handle non-finite values.
Results may differ from a plain program's by a relative error of at most 0.0075.
Values may be sent and summed in bfloat16 or wider, within the bound.
No kernel may reach another device: no remote copies, remote signals or barrier semaphores. Data moves between devices by JAX's collectives and lax.ppermute only.
A program may use at most 64 MiB of HBM per device.

v0:
```python
import jax
import jax.numpy as jnp
from jax import lax
from jax.sharding import PartitionSpec as P

SEQ = 64
masked_fill = -1e30


def body(hidden, embedding, block_counts, lang_blocks, sent_lang, targets):
    tok_dev = hidden.shape[0]
    vocab_count = lax.axis_size("vocab")
    batch_count = lax.axis_size("batch")
    vocab_index = lax.axis_index("vocab")
    batch_index = lax.axis_index("batch")
    local_rows = embedding.shape[0]
    local_blocks = block_counts.shape[0]
    block_width = local_rows // local_blocks
    gathered = lax.all_gather(hidden, "vocab", axis=0, tiled=True)
    token_count = gathered.shape[0]
    token_ids = (
        (jnp.arange(vocab_count, dtype=jnp.int32)[:, None] * batch_count + batch_index) * tok_dev
        + jnp.arange(tok_dev, dtype=jnp.int32)[None, :]
    ).reshape(-1)
    target_ids = lax.dynamic_index_in_dim(
        targets.reshape(vocab_count, batch_count, tok_dev), batch_index, 1, keepdims=False
    ).reshape(-1)
    sentence = token_ids // SEQ
    sentence_hit = sentence[:, None] == jnp.arange(sent_lang.shape[0], dtype=jnp.int32)[None, :]
    token_language = jnp.sum(jnp.where(sentence_hit, sent_lang[None, :], 0), axis=1)
    block_ids = vocab_index * local_blocks + jnp.arange(local_blocks, dtype=jnp.int32)
    member = jnp.any(lang_blocks[:, :, None] == block_ids[None, None, :], axis=1).astype(
        jnp.float32
    )
    language_hit = (
        token_language[:, None] == jnp.arange(lang_blocks.shape[0], dtype=jnp.int32)[None, :]
    ).astype(jnp.float32)
    allowed = jnp.dot(language_hit, member, precision=lax.Precision.HIGHEST) > 0.5
    allowed_cells = allowed[:, :, None]
    raw_scores = lax.dot_general(
        gathered, embedding, (((1,), (1,)), ((), ())), preferred_element_type=jnp.float32
    )
    log_sampling = jnp.log(block_counts.astype(jnp.float32))
    logits = (
        raw_scores.reshape(token_count, local_blocks, block_width) - log_sampling[None, :, None]
    )
    masked = jnp.where(allowed_cells, logits, masked_fill)
    word_ids = (vocab_index * local_rows + jnp.arange(local_rows, dtype=jnp.int32)).reshape(
        local_blocks, block_width
    )
    is_target = word_ids[None, :, :] == target_ids[:, None, None]
    local_peak = jnp.max(masked, axis=(1, 2))
    local_target = jnp.sum(jnp.where(is_target, logits, 0.0), axis=(1, 2))
    peak_value = lax.pmax(local_peak, "vocab")
    local_total = jnp.sum(
        jnp.where(allowed_cells, jnp.exp(masked - peak_value[:, None, None]), 0.0), axis=(1, 2)
    )
    denominator, target_logit = lax.psum((local_total, local_target), "vocab")
    log_total = peak_value + jnp.log(denominator)
    every_loss = log_total - target_logit
    token_loss = lax.dynamic_slice_in_dim(every_loss, vocab_index * tok_dev, tok_dev, 0)
    softmax_weights = jnp.where(allowed_cells, jnp.exp(logits - log_total[:, None, None]), 0.0)
    grad_logits = (
        (softmax_weights - is_target.astype(jnp.float32))
        .astype(jnp.bfloat16)
        .reshape(token_count, local_rows)
    )
    columns = lax.all_to_all(grad_logits, "batch", split_axis=1, concat_axis=0, tiled=True)
    everyone = lax.all_gather(gathered, "batch", axis=0, tiled=True)
    summed = jnp.zeros((columns.shape[1], gathered.shape[1]), jnp.float32)
    for source in range(batch_count):
        slice_grad = columns[source * token_count : (source + 1) * token_count]
        slice_rows = everyone[source * token_count : (source + 1) * token_count]
        contribution = lax.dot_general(
            slice_grad, slice_rows, (((0,), (0,)), ((), ())), preferred_element_type=jnp.float32
        )
        rounded = lax.optimization_barrier(contribution.astype(jnp.bfloat16))
        summed = summed + rounded.astype(jnp.float32)
    grad_embed = summed.astype(jnp.bfloat16)
    return (token_loss, grad_embed)


def solution(mesh):
    in_specs = (P(("vocab", "batch"), None), P("vocab", None), P("vocab"), P(), P(), P())
    out_specs = (P(("vocab", "batch")), P(("vocab", "batch"), None))
    return jax.shard_map(body, mesh=mesh, in_specs=in_specs, out_specs=out_specs, check_vma=False)
```

profile of v0, /device:TPU:0, one launch (start us, length us, event | category | flops | bytes accessed | tf_op | source)
XLA Modules:
  0.0 92.3 jit_solution(3741572874803002125)
XLA Ops:
  0.6 0.0 copy-start
  0.7 0.8 convert_log_fusion
  1.5 0.1 broadcast_bitcast_fusion
  1.6 0.1 iota_add_fusion
  1.6 0.1 add.93
  1.7 1.0 %compare_reduce_fusion = pred[200,8]{0,1:T(8,128)(4,1)S(1)} fusion(s32[200,64]{0,1:T(8,128)} %param.9, s32[8]{0:T(128)S(1)} %iota_add_fusion.1), kind=kLoop, calls=%fused_computation.7 | loop fusion | flops 203200 | bytes 52832 | tf_op jit(solution)/shard_map/reduce_or | solution.py:32
  2.7 0.7 select_reduce_fusion.1
  3.5 0.2 convolution_compare_fusion
  3.7 0.1 copy.13
  3.8 0.8 reshape.91
  4.6 0.1 eq.66
  4.7 32.5 %all_gather.6 = bf16[64,1024]{1,0:T(8,128)(2,1)S(1)} all-gather(bf16[8,1024]{1,0:T(8,128)(2,1)} %param.6), channel_id=1, replica_groups=mesh['vocab'=8,'batch'=4] {'vocab'}, dimensions={0}, use_global_device_ids=true | all-gather | bytes 147456 | tf_op jit(solution)/shard_map/all_gather | solution.py:19
  37.2 0.1 broadcast_in_dim.53
  37.3 0.0 copy-done
  37.3 0.9 fusion.3
  38.2 21.3 %pmax.7 = f32[64]{0:T(128)S(1)} all-reduce(f32[64]{0:T(128)S(1)} %get-tuple-element.8), channel_id=1, replica_groups=mesh['vocab'=8,'batch'=4] {'vocab'}, use_global_device_ids=true, to_apply=%region_3.4 | all-reduce | flops 64 | bytes 512 | tf_op jit(solution)/shard_map/pmax | solution.py:54
  59.5 0.3 fusion
  59.8 17.1 %all-reduce = (f32[64]{0:T(128)S(1)}, f32[64]{0:T(128)S(1)}) all-reduce(f32[64]{0:T(128)S(1)} %get-tuple-element.3, f32[64]{0:T(128)S(1)} %get-tuple-element.2), channel_id=1, replica_groups=mesh['vocab'=8,'batch'=4] {'vocab'}, use_global_device_ids=true, to_apply=%region_5.6 | all-reduce | flops 128 | bytes 1024 | tf_op jit(solution)/shard_map/psum | solution.py:58
  76.9 0.1 fusion.2
  77.1 0.7 copy.21
  77.7 3.3 %all-to-all-start = ((bf16[64,4,256]{2,0,1:T(8,128)(2,1)}), bf16[64,4,256]{2,0,1:T(8,128)(2,1)S(1)}, u32[]{:S(2)}, u32[]{:S(2)}) async-start(bf16[64,4,256]{2,0,1:T(8,128)(2,1)} %bitcast.32), calls=%async_computation | async-start | bytes 262144 | tf_op jit(solution)/shard_map/all_to_all | solution.py:68
  81.1 8.2 %all_gather.7 = bf16[256,1024]{1,0:T(8,128)(2,1)S(1)} all-gather(bf16[64,1024]{1,0:T(8,128)(2,1)S(1)} %all_gather.6), channel_id=1, replica_groups=mesh['vocab'=8,'batch'=4] {'batch'}, dimensions={0}, use_global_device_ids=true | all-gather | bytes 655360 | tf_op jit(solution)/shard_map/all_gather | solution.py:69
  89.3 0.6 dynamic_slice.8
  89.9 0.0 all-to-all-done
  89.9 0.3 convolution_convert_fusion
  90.2 0.3 convolution_convert_fusion.1
  90.5 0.3 convolution_convert_fusion.2
  90.9 0.3 convolution_convert_fusion.3
  91.2 1.1 %add_convert_fusion = bf16[256,1024]{1,0:T(8,128)(2,1)} fusion(bf16[256,1024]{1,0:T(8,128)(2,1)S(1)} %convolution_convert_fusion, bf16[256,1024]{1,0:T(8,128)(2,1)S(1)} %convolution_convert_fusion.1, bf16[256,1024]{1,0:T(8,128)(2,1)S(1)} %convolution_convert_fusion.2, bf16[256,1024]{1,0:T(8,128)(2,1)S(1)} %convolution_convert_fusion.3), kind=kLoop, calls=%fused_computation.6 | loop fusion | flops 2097152 | bytes 2621440 | tf_op jit(solution)/shard_map/convert_element_type | solution.py:79
  (6 shorter events, 0.1 us)
Async XLA Ops:
  0.6 36.7 %copy-start = (bf16[1024,1024]{1,0:T(8,128)(2,1)S(1)}, bf16[1024,1024]{1,0:T(8,128)(2,1)}, u32[]{:S(2)}) copy-start(bf16[1024,1024]{1,0:T(8,128)(2,1)} %param.7) | copy-start | bytes 6291460
  77.7 12.2 %all-to-all-start = ((bf16[64,4,256]{2,0,1:T(8,128)(2,1)}), bf16[64,4,256]{2,0,1:T(8,128)(2,1)S(1)}, u32[]{:S(2)}, u32[]{:S(2)}) async-start(bf16[64,4,256]{2,0,1:T(8,128)(2,1)} %bitcast.32), calls=%async_computation | async-start | bytes 262144 | tf_op jit(solution)/shard_map/all_to_all | solution.py:68
where the time goes:
time: 92.7 us; the launch traced here: 92.3 us
  blocking collectives  79.2 us (85%)
  other arithmetic  4.2 us (5%)
  starting transfers between devices  3.33 us (4%)
  local copies, waits for them, and re-layouts  2.52 us (3%)
  matrix products  2.32 us (3%)
    all_gather x1, blocking collectives, body(): gathered = lax.all_gather(hidden, 'vocab', axis=0, tiled=True)  32.5 us
    pmax x1, blocking collectives, body(): peak_value = lax.pmax(local_peak, 'vocab')  21.3 us
    psum x1, blocking collectives, body(): denominator, target_logit = lax.psum((local_total, local_target), 'vocab')  17.1 us
    all_gather x1, blocking collectives, body(): everyone = lax.all_gather(gathered, 'batch', axis=0, tiled=True)  8.24 us
    all_to_all x1, starting transfers between devices, body(): lax.all_to_all(grad_logits, 'batch', split_axis=1, concat_axis=0, tiled=T...  3.33 us
  transfers between devices with their start and end apart: 1, of which 0 were waited for; matrix products, arithmetic and copies ran while one was open for 1% of the time, Pallas kernels for 0%

commit v1 on v0

--- a/solution.py
+++ b/solution.py
@@ -66,7 +66,14 @@
         .reshape(token_count, local_rows)
     )
     columns = lax.all_to_all(grad_logits, "batch", split_axis=1, concat_axis=0, tiled=True)
-    everyone = lax.all_gather(gathered, "batch", axis=0, tiled=True)
+    ring = [gathered]
+    for hop in range(3):
+        ring.append(lax.ppermute(ring[-1], "batch", [(dev, (dev + 1) % 4) for dev in range(4)]))
+    everyone = jnp.roll(
+        jnp.concatenate(ring[::-1], axis=0),
+        (lax.axis_index("batch") + 1) * ring[0].shape[0],
+        axis=0,
+    )
     summed = jnp.zeros((columns.shape[1], gathered.shape[1]), jnp.float32)
     for source in range(batch_count):
         slice_grad = columns[source * token_count : (source + 1) * token_count]

time: 92.7 us -> 99 us (1.068); the launches traced: 92.3 us -> 97.4 us
  blocking collectives: 79.2 us -> 71.1 us
  local copies, waits for them, and re-layouts: 2.52 us -> 7.8 us
  waiting for transfers between devices: 0.01 us -> 4.37 us
  matrix products: 2.32 us -> 5.95 us
    all_gather x1 -> x0, blocking collectives: 8.24 us -> none  [body(): everyone = lax.all_gather(gathered, 'batch', axis=0, tiled=True)]
    unnamed x2 -> x9, local copies, waits for them, and re-layouts: 0.01 us -> 4.61 us
    ppermute x0 -> x3, waiting for transfers between devices: none -> 4.37 us  [body(): lax.ppermute(ring[-1], 'batch', [(dev, (dev + 1) % 4) for dev in range(4)])]
    dot_general x4, matrix products: 1.25 us -> 4.88 us  [body(): lax.dot_general(slice_grad, slice_rows, (((0,), (0,)), ((), ())), preferr...]
  transfers between devices with their start and end apart: 1 -> 4, of which waited for: 0 -> 1; matrix products, arithmetic and copies ran while one was open for 1% -> 12% of each run, Pallas kernels for 0% -> 0%
where the time goes in v1:
time: 99 us; the launch traced here: 97.4 us
  blocking collectives  71.1 us (72%)
  local copies, waits for them, and re-layouts  7.8 us (8%)
  matrix products  5.95 us (6%)
  waiting for transfers between devices  4.37 us (4%)
  other arithmetic  4.05 us (4%)
  starting transfers between devices  3.38 us (3%)
    all_gather x1, blocking collectives, body(): gathered = lax.all_gather(hidden, 'vocab', axis=0, tiled=True)  32.7 us
    pmax x1, blocking collectives, body(): peak_value = lax.pmax(local_peak, 'vocab')  21.3 us
    psum x1, blocking collectives, body(): denominator, target_logit = lax.psum((local_total, local_target), 'vocab')  17.1 us
    dot_general x4, matrix products, body(): lax.dot_general(slice_grad, slice_rows, (((0,), (0,)), ((), ())), preferr...  4.88 us
    unnamed x9, local copies, waits for them, and re-layouts  4.61 us
    ppermute x3, waiting for transfers between devices, body(): lax.ppermute(ring[-1], 'batch', [(dev, (dev + 1) % 4) for dev in range(4)])  4.37 us
    all_to_all x1, starting transfers between devices, body(): lax.all_to_all(grad_logits, 'batch', split_axis=1, concat_axis=0, tiled=T...  3.33 us
  transfers between devices with their start and end apart: 4, of which 1 were waited for; matrix products, arithmetic and copies ran while one was open for 12% of the time, Pallas kernels for 0%

profile of v1, /device:TPU:0, one launch (start us, length us, event | category | flops | bytes accessed | tf_op | source)
XLA Modules:
  0.0 97.4 jit_solution(7140299390625155706)
XLA Ops:
  0.6 0.0 copy-start
  0.6 32.7 %all_gather.3 = bf16[64,1024]{1,0:T(8,128)(2,1)S(1)} all-gather(bf16[8,1024]{1,0:T(8,128)(2,1)} %param.6), channel_id=1, replica_groups=mesh['vocab'=8,'batch'=4] {'vocab'}, dimensions={0}, use_global_device_ids=true | all-gather | bytes 147456 | tf_op jit(solution)/shard_map/all_gather | solution.py:19
  33.3 0.0 collective-permute-start
  33.4 0.7 convert_log_fusion
  34.0 0.1 broadcast_bitcast_fusion
  34.1 0.1 iota_add_fusion
  34.2 0.1 add.106
  34.3 1.0 %compare_reduce_fusion = pred[200,8]{0,1:T(8,128)(4,1)S(1)} fusion(s32[200,64]{0,1:T(8,128)} %param.9, s32[8]{0:T(128)S(1)} %iota_add_fusion.1), kind=kLoop, calls=%fused_computation.7 | loop fusion | flops 203200 | bytes 52832 | tf_op jit(solution)/shard_map/reduce_or | solution.py:32
  35.3 0.7 select_reduce_fusion.1
  36.0 0.2 convolution_compare_fusion
  36.2 0.1 copy.13
  36.3 0.8 reshape.91
  37.1 0.1 eq.69
  37.2 0.1 broadcast_in_dim.53
  37.3 0.0 copy-done
  37.4 0.9 fusion.3
  38.2 21.3 %pmax.7 = f32[64]{0:T(128)S(1)} all-reduce(f32[64]{0:T(128)S(1)} %get-tuple-element.8), channel_id=1, replica_groups=mesh['vocab'=8,'batch'=4] {'vocab'}, use_global_device_ids=true, to_apply=%region_3.4 | all-reduce | flops 64 | bytes 512 | tf_op jit(solution)/shard_map/pmax | solution.py:54
  59.5 0.3 fusion
  59.8 17.1 %all-reduce = (f32[64]{0:T(128)S(1)}, f32[64]{0:T(128)S(1)}) all-reduce(f32[64]{0:T(128)S(1)} %get-tuple-element.3, f32[64]{0:T(128)S(1)} %get-tuple-element.2), channel_id=1, replica_groups=mesh['vocab'=8,'batch'=4] {'vocab'}, use_global_device_ids=true, to_apply=%region_5.6 | all-reduce | flops 128 | bytes 1024 | tf_op jit(solution)/shard_map/psum | solution.py:58
  76.9 0.0 collective-permute-done
  76.9 0.0 collective-permute-start.1
  77.0 4.4 %collective-permute-done.1 = bf16[64,1024]{1,0:T(8,128)(2,1)S(1)} collective-permute-done((bf16[64,1024]{1,0:T(8,128)(2,1)S(1)}, bf16[64,1024]{1,0:T(8,128)(2,1)S(1)}, u32[]{:S(2)}, u32[]{:S(2)}) %collective-permute-start.1) | collective-permute-done | bytes 131104 | tf_op jit(solution)/shard_map/ppermute | solution.py:71
  81.3 0.0 collective-permute-start.2
  81.3 0.1 fusion.2
  81.5 0.7 copy.21
  82.2 3.3 %all-to-all-start = ((bf16[64,4,256]{2,0,1:T(8,128)(2,1)}), bf16[64,4,256]{2,0,1:T(8,128)(2,1)S(1)}, u32[]{:S(2)}, u32[]{:S(2)}) async-start(bf16[64,4,256]{2,0,1:T(8,128)(2,1)} %bitcast.32), calls=%async_computation | async-start | bytes 262144 | tf_op jit(solution)/shard_map/all_to_all | solution.py:68
  85.5 0.6 dynamic_slice.12
  86.1 0.0 collective-permute-done.2
  86.1 0.6 constant_dynamic-update-slice_fusion.7
  86.7 0.7 constant_dynamic-update-slice_fusion.6
  87.4 0.7 constant_dynamic-update-slice_fusion.5
  88.1 0.7 constant_dynamic-update-slice_fusion.4
  88.7 0.7 constant_dynamic-update-slice_fusion.3
  89.4 0.6 constant_dynamic-update-slice_fusion.2
  90.0 0.7 constant_dynamic-update-slice_fusion.1
  90.7 0.7 constant_dynamic-update-slice_fusion
  91.4 0.0 all-to-all-done
  91.4 1.2 %convolution_convert_fusion.3 = bf16[256,1024]{1,0:T(8,128)(2,1)S(1)} fusion(bf16[512,1024]{1,0:T(8,128)(2,1)} %constant_dynamic-update-slice_fusion, s32[]{:T(128)S(6)} %select_n.61, bf16[4,64,256]{2,1,0:T(8,128)(2,1)S(1)} %bitcast.36), kind=kOutput, calls=%fused_computation.3 | convolution fusion | flops 33816576 | bytes 688132 | tf_op jit(solution)/shard_map/dot_general | solution.py:81
  92.6 1.2 %convolution_convert_fusion.1 = bf16[256,1024]{1,0:T(8,128)(2,1)S(1)} fusion(bf16[512,1024]{1,0:T(8,128)(2,1)} %constant_dynamic-update-slice_fusion, s32[]{:T(128)S(6)} %add.124, bf16[4,64,256]{2,1,0:T(8,128)(2,1)S(1)} %bitcast.37), kind=kOutput, calls=%fused_computation.1 | convolution fusion | flops 33816576 | bytes 688132 | tf_op jit(solution)/shard_map/dot_general | solution.py:81
  93.8 1.2 %convolution_convert_fusion.2 = bf16[256,1024]{1,0:T(8,128)(2,1)S(1)} fusion(bf16[512,1024]{1,0:T(8,128)(2,1)} %constant_dynamic-update-slice_fusion, s32[]{:T(128)S(6)} %add.123, bf16[4,64,256]{2,1,0:T(8,128)(2,1)S(1)} %bitcast.38), kind=kOutput, calls=%fused_computation.2 | convolution fusion | flops 33816576 | bytes 688132 | tf_op jit(solution)/shard_map/dot_general | solution.py:81
  95.1 1.2 %convolution_convert_fusion = bf16[256,1024]{1,0:T(8,128)(2,1)S(1)} fusion(bf16[512,1024]{1,0:T(8,128)(2,1)} %constant_dynamic-update-slice_fusion, s32[]{:T(128)S(6)} %add.125, bf16[4,64,256]{2,1,0:T(8,128)(2,1)S(1)} %bitcast.39), kind=kOutput, calls=%fused_computation | convolution fusion | flops 33816576 | bytes 688132 | tf_op jit(solution)/shard_map/dot_general | solution.py:81
  96.3 1.1 %add_convert_fusion = bf16[256,1024]{1,0:T(8,128)(2,1)} fusion(bf16[256,1024]{1,0:T(8,128)(2,1)S(1)} %convolution_convert_fusion, bf16[256,1024]{1,0:T(8,128)(2,1)S(1)} %convolution_convert_fusion.1, bf16[256,1024]{1,0:T(8,128)(2,1)S(1)} %convolution_convert_fusion.2, bf16[256,1024]{1,0:T(8,128)(2,1)S(1)} %convolution_convert_fusion.3), kind=kLoop, calls=%fused_computation.6 | loop fusion | flops 2097152 | bytes 2621440 | tf_op jit(solution)/shard_map/convert_element_type | solution.py:86
  (6 shorter events, 0.1 us)
Async XLA Ops:
  0.6 36.7 %copy-start = (bf16[1024,1024]{1,0:T(8,128)(2,1)S(1)}, bf16[1024,1024]{1,0:T(8,128)(2,1)}, u32[]{:S(2)}) copy-start(bf16[1024,1024]{1,0:T(8,128)(2,1)} %param.7) | copy-start | bytes 6291460
  33.3 43.6 %collective-permute-start = (bf16[64,1024]{1,0:T(8,128)(2,1)S(1)}, bf16[64,1024]{1,0:T(8,128)(2,1)S(1)}, u32[]{:S(2)}, u32[]{:S(2)}) collective-permute-start(bf16[64,1024]{1,0:T(8,128)(2,1)S(1)} %all_gather.3), channel_id=1, source_target_pairs={{0,1},{1,2},{2,3},{3,0},{4,5},{5,6},{6,7},{7,4},{8,9},{9,10},{10,1... | collective-permute-start | bytes 393224 | tf_op jit(solution)/shard_map/ppermute | solution.py:71
  76.9 4.4 %collective-permute-start.1 = (bf16[64,1024]{1,0:T(8,128)(2,1)S(1)}, bf16[64,1024]{1,0:T(8,128)(2,1)S(1)}, u32[]{:S(2)}, u32[]{:S(2)}) collective-permute-start(bf16[64,1024]{1,0:T(8,128)(2,1)S(1)} %collective-permute-done), channel_id=1, source_target_pairs={{0,1},{1,2},{2,3},{3,0},{4,5},{5,6},{6,7},{7,4},{8,9},{9,10},{10,1... | collective-permute-start | bytes 393224 | tf_op jit(solution)/shard_map/ppermute | solution.py:71
  81.3 4.8 %collective-permute-start.2 = (bf16[64,1024]{1,0:T(8,128)(2,1)S(1)}, bf16[64,1024]{1,0:T(8,128)(2,1)S(1)}, u32[]{:S(2)}, u32[]{:S(2)}) collective-permute-start(bf16[64,1024]{1,0:T(8,128)(2,1)S(1)} %collective-permute-done.1), channel_id=1, source_target_pairs={{0,1},{1,2},{2,3},{3,0},{4,5},{5,6},{6,7},{7,4},{8,9},{9,10},{10,1... | collective-permute-start | bytes 393224 | tf_op jit(solution)/shard_map/ppermute | solution.py:71
  82.2 9.2 %all-to-all-start = ((bf16[64,4,256]{2,0,1:T(8,128)(2,1)}), bf16[64,4,256]{2,0,1:T(8,128)(2,1)S(1)}, u32[]{:S(2)}, u32[]{:S(2)}) async-start(bf16[64,4,256]{2,0,1:T(8,128)(2,1)} %bitcast.32), calls=%async_computation | async-start | bytes 262144 | tf_op jit(solution)/shard_map/all_to_all | solution.py:68
